TPU v7x, 32 devices: a whole 2x2x4 slice. The times are simulated.
32 devices in a mesh: wide: 8 (over z, y), narrow: 4 (over x, core).
Axes of the slice: x: 2, y: 2, z: 4, core: 2. Of those that a mesh axis runs over, the one named last changes fastest.
Arguments:
- desc_a: bfloat16 [4096, 128], P('wide'), may hold values from -6 to 6
- desc_b: bfloat16 [32768, 128], P('narrow'), may hold values from -6 to 6
- logmass_a: float32 [4096], P('wide'), may hold values from -6 to 6
- logmass_b: float32 [32768], P('narrow'), may hold values from -6 to 6
- g_start: float32 [32768], P('narrow'), may hold values from -1 to 16, as said below
Outputs:
- potential_a: float32 [4096], P('wide')
- potential_b: float32 [32768], P('narrow')
- flow_a: float32 [4096, 128], P('wide')
- flow_b: float32 [32768, 128], P(('narrow', 'wide'))
Inputs may be any that keep to these rules, and one draw needn't show every extreme that they name: `g_start`: potentials of view B carried over from the previous pair of views.
All inputs are finite; a program needn't handle non-finite values.
Results may differ from a plain program's by a relative error of at most 0.01.
Values may be sent and summed in bfloat16 or wider, within the bound.
A program may use at most 64 MiB of HBM per device.

v0:
```python
import jax
import jax.numpy as jnp
from jax import lax
from jax.sharding import PartitionSpec as P

ITERS = 2


EPS = 0.05


def combined_all(part, axis, combine):
    gathered = jax.tree.map(lambda a: lax.all_gather(a, axis), part)

    def take(source):
        return jax.tree.map(lambda a: lax.dynamic_index_in_dim(a, source, 0, False), gathered)

    return lax.fori_loop(
        1, lax.axis_size(axis), lambda source, state: combine(state, take(source)), take(0)
    )


def unit_rows(desc):
    wide32 = desc.astype(jnp.float32)
    return (wide32 / jnp.sqrt(jnp.sum(wide32 * wide32, axis=1, keepdims=True) + 1e-06)).astype(
        jnp.bfloat16
    )


def cost_of(left, right):
    return 2.0 - 2.0 * lax.dot_general(
        left, right, (((1,), (1,)), ((), ())), preferred_element_type=jnp.float32
    )


def left_product(weights, tile_a):
    return lax.dot_general(
        weights, tile_a, (((0,), (0,)), ((), ())), preferred_element_type=jnp.float32
    )


def pair_combine(first_pair, second_pair):
    new_high = jnp.maximum(first_pair[0], second_pair[0])
    summed = first_pair[1] * jnp.exp(first_pair[0] - new_high) + second_pair[1] * jnp.exp(
        second_pair[0] - new_high
    )
    return (new_high, summed)


def finish_rows(highest, summed):
    highest, summed = combined_all((highest, summed), "narrow", pair_combine)
    return highest + jnp.log(summed)


def finish_cols(highest, summed):
    highest, summed = combined_all((highest, summed), "wide", pair_combine)
    return highest + jnp.log(summed)


def row_update(state_now, pot_part, cost):
    highest, summed = state_now
    scores = (pot_part[None, :] - cost) / EPS
    new_high = jnp.maximum(highest, jnp.max(scores, axis=1))
    summed = summed * jnp.exp(highest - new_high) + jnp.sum(
        jnp.exp(scores - new_high[:, None]), axis=1
    )
    return (new_high, summed)


def on_device(desc_a, desc_b, logmass_a, logmass_b, g_start):
    unit_a = unit_rows(desc_a)
    unit_b = unit_rows(desc_b)
    n_rows, feat_width = unit_a.shape
    n_cols = unit_b.shape[0]
    col_span = min(n_cols, 2048)
    n_tiles = n_cols // col_span
    b_tiles = unit_b.reshape(n_tiles, col_span, feat_width)
    row_init = (jnp.full((n_rows,), -jnp.inf, jnp.float32), jnp.zeros((n_rows,), jnp.float32))

    def row_partial(potential):

        def row_one_tile(state_now, inputs):
            tile_b, pot_part = inputs
            return (row_update(state_now, pot_part, cost_of(unit_a, tile_b)), None)

        result, _ = lax.scan(
            row_one_tile, row_init, (b_tiles, potential.reshape(n_tiles, col_span))
        )
        return result

    potential_b = g_start
    for sweep_index in range(ITERS):
        row_pot = EPS * logmass_a - EPS * finish_rows(*row_partial(potential_b))

        def col_one_tile(tile_b):
            scores = (row_pot[:, None] - cost_of(unit_a, tile_b)) / EPS
            highest = jnp.max(scores, axis=0)
            return (highest, jnp.sum(jnp.exp(scores - highest[None, :]), axis=0))

        highest, summed = lax.map(col_one_tile, b_tiles)
        lse_b = finish_cols(*(highest.reshape(n_cols), summed.reshape(n_cols)))
        potential_b = EPS * logmass_b - EPS * lse_b
    my_share = n_cols // lax.axis_size("wide")
    first_row = lax.axis_index("wide") * my_share
    own_cols = lax.dynamic_slice_in_dim(unit_b, first_row, my_share, 0)

    def joint_tile(state_now, inputs):
        tile_b, pot_part, lse_part = inputs
        cost = cost_of(unit_a, tile_b)
        weights = jnp.exp((row_pot[:, None] - cost) / EPS - lse_part[None, :]).astype(jnp.bfloat16)
        return (row_update(state_now, pot_part, cost), left_product(weights, unit_a))

    row_stats, tile_sums = lax.scan(
        joint_tile,
        row_init,
        (b_tiles, potential_b.reshape(n_tiles, col_span), lse_b.reshape(n_tiles, col_span)),
    )
    lse_a = finish_rows(*row_stats)
    sums_b = lax.psum_scatter(
        tile_sums.reshape(n_cols, feat_width).astype(jnp.bfloat16),
        "wide",
        scatter_dimension=0,
        tiled=True,
    ).astype(jnp.float32)
    flow_b = sums_b - own_cols.astype(jnp.float32)
    potential_a = EPS * logmass_a - EPS * lse_a

    def flow_tile(acc_now, inputs):
        tile_b, pot_part = inputs
        weights = jnp.exp(
            (pot_part[None, :] - cost_of(unit_a, tile_b)) / EPS - lse_a[:, None]
        ).astype(jnp.bfloat16)
        return (acc_now + jnp.dot(weights, tile_b, preferred_element_type=jnp.float32), None)

    sums_a, _ = lax.scan(
        flow_tile,
        jnp.zeros((n_rows, feat_width), jnp.float32),
        (b_tiles, potential_b.reshape(n_tiles, col_span)),
    )
    sums_a = lax.psum(sums_a.astype(jnp.bfloat16), "narrow").astype(jnp.float32)
    flow_a = sums_a - unit_a.astype(jnp.float32)
    return (potential_a, potential_b, flow_a, flow_b)


def solution(mesh):
    return jax.shard_map(
        on_device,
        mesh=mesh,
        in_specs=(P("wide", None), P("narrow", None), P("wide"), P("narrow"), P("narrow")),
        out_specs=(P("wide"), P("narrow"), P("wide", None), P(("narrow", "wide"), None)),
        check_vma=False,
    )
```

profile of v0, /device:TPU:1, one launch (start us, length us, event | category | flops | bytes accessed | tf_op | source)
XLA Modules:
  0.0 358.3 jit_solution(10728813550272672152)
XLA Ops:
  8.1 2.7 fusion.36
  10.9 4.6 %fusion.37 = bf16[8192,128]{1,0:T(8,128)(2,1)S(1)} fusion(bf16[8192,128]{1,0:T(8,128)(2,1)} %param.28, f32[8192]{0:T(1024)S(1)} %add_sqrt_fusion), kind=kLoop, calls=%fused_computation.76 | loop fusion | flops 3145728 | bytes 4227072 | tf_op jit(solution)/shard_map/convert_element_type | solution.py:25
  15.8 22.7 %while.168 = (s32[]{:T(128)}, f32[512]{0:T(512)S(1)}, f32[512]{0:T(512)S(1)}, f32[4,2048]{1,0:T(4,128)S(1)}, bf16[4,2048,128]{2,1,0:T(8,128)(2,1)S(1)}, /*index=5*/bf16[512,128]{1,0:T(8,128)(2,1)S(1)}, s32[]{:T(128)}, s32[]{:T(128)}) while((s32[]{:T(128)}, f32[512]{0:T(512)S(1)}, f32[512]{0:T(512)S(1)}, f32[4,2048]{1,0:T(4,128)S(1)}, ...), condition=%wide.region_5.6_spmd.clone, body=%wide.region_2.5_spmd.clone.sunk | while | flops 275778048 | bytes 9095272 | solution.py:86
  15.9 2.8 fusion.75
  18.7 2.8 exponential_reduce_fusion.12
  21.6 2.8 fusion.75
  24.3 2.8 exponential_reduce_fusion.12
  27.2 2.8 fusion.75
  30.0 2.8 exponential_reduce_fusion.12
  32.9 2.8 fusion.75
  35.7 2.8 exponential_reduce_fusion.12
  38.5 6.0 %all-gather.6 = f32[4,1,512]{2,1,0:T(1,128)S(1)} all-gather(f32[1,1,512]{2,1,0:T(1,128)S(1)} %bitcast.198), channel_id=2, replica_groups=mesh['wide'=8,'narrow'=4] {'narrow'}, dimensions={0}, use_global_device_ids=true | all-gather | bytes 10240 | tf_op jit(solution)/shard_map/all_gather | solution.py:13
  44.6 5.5 %all-gather.7 = f32[4,1,512]{2,1,0:T(1,128)S(1)} all-gather(f32[1,1,512]{2,1,0:T(1,128)S(1)} %bitcast.217), channel_id=3, replica_groups=mesh['wide'=8,'narrow'=4] {'narrow'}, dimensions={0}, use_global_device_ids=true | all-gather | bytes 10240 | tf_op jit(solution)/shard_map/all_gather | solution.py:13
  50.3 7.3 %while.162 = (s32[]{:T(128)}, f32[4,2048]{1,0:T(4,128)S(1)}, f32[4,2048]{1,0:T(4,128)S(1)}, f32[512]{0:T(512)S(1)}, bf16[4,2048,128]{2,1,0:T(8,128)(2,1)S(1)}, /...) while((s32[]{:T(128)}, f32[4,2048]{1,0:T(4,128)S(1)}, f32[4,2048]{1,0:T(4,128)S(1)}, ...), condition=%wide.region_11.12_spmd, body=%wide.region_8.11_spmd.sunk | while | flops 275771392 | bytes 9103457 | solution.py:100
  57.6 24.9 %all-gather.8 = f32[8,1,8192]{2,1,0:T(1,128)S(1)} all-gather(f32[1,1,8192]{2,1,0:T(1,128)S(1)} %reshape.74), channel_id=1, replica_groups=mesh['wide'=8,'narrow'=4] {'wide'}, dimensions={0}, use_global_device_ids=true | all-gather | bytes 294912 | tf_op jit(solution)/shard_map/all_gather | solution.py:13
  82.8 24.6 %all-gather.9 = f32[8,1,8192]{2,1,0:T(1,128)S(1)} all-gather(f32[1,1,8192]{2,1,0:T(1,128)S(1)} %reshape.76), channel_id=1, replica_groups=mesh['wide'=8,'narrow'=4] {'wide'}, dimensions={0}, use_global_device_ids=true | all-gather | bytes 294912 | tf_op jit(solution)/shard_map/all_gather | solution.py:13
  108.5 22.7 %while.169 = (s32[]{:T(128)}, f32[512]{0:T(512)S(1)}, f32[512]{0:T(512)S(1)}, f32[4,2048]{1,0:T(4,128)S(1)}, bf16[4,2048,128]{2,1,0:T(8,128)(2,1)S(1)}, /*index=5*/bf16[512,128]{1,0:T(8,128)(2,1)S(1)}, s32[]{:T(128)}, s32[]{:T(128)}) while((s32[]{:T(128)}, f32[512]{0:T(512)S(1)}, f32[512]{0:T(512)S(1)}, ...), condition=%wide.region_17.18_spmd.clone, body=%wide.region_14.17_spmd.clone.sunk | while | flops 275778048 | bytes 9095272 | solution.py:86
  108.5 2.8 fusion.78
  111.3 2.8 exponential_reduce_fusion.13
  114.2 2.8 fusion.78
  117.0 2.8 exponential_reduce_fusion.13
  119.8 2.8 fusion.78
  122.6 2.8 exponential_reduce_fusion.13
  125.5 2.8 fusion.78
  128.3 2.8 exponential_reduce_fusion.13
  131.1 17.8 %all-gather.10 = f32[4,1,512]{2,1,0:T(1,128)S(1)} all-gather(f32[1,1,512]{2,1,0:T(1,128)S(1)} %bitcast.197), channel_id=4, replica_groups=mesh['wide'=8,'narrow'=4] {'narrow'}, dimensions={0}, use_global_device_ids=true | all-gather | bytes 10240 | tf_op jit(solution)/shard_map/all_gather | solution.py:13
  149.0 5.2 %all-gather.11 = f32[4,1,512]{2,1,0:T(1,128)S(1)} all-gather(f32[1,1,512]{2,1,0:T(1,128)S(1)} %bitcast.216), channel_id=5, replica_groups=mesh['wide'=8,'narrow'=4] {'narrow'}, dimensions={0}, use_global_device_ids=true | all-gather | bytes 10240 | tf_op jit(solution)/shard_map/all_gather | solution.py:13
  154.4 7.3 %while.165 = (s32[]{:T(128)}, f32[4,2048]{1,0:T(4,128)S(1)}, f32[4,2048]{1,0:T(4,128)S(1)}, f32[512]{0:T(512)S(1)}, bf16[4,2048,128]{2,1,0:T(8,128)(2,1)S(1)}, /...) while((s32[]{:T(128)}, f32[4,2048]{1,0:T(4,128)S(1)}, f32[4,2048]{1,0:T(4,128)S(1)}, ...), condition=%wide.region_23.24_spmd, body=%wide.region_20.23_spmd.sunk | while | flops 275771392 | bytes 9103457 | solution.py:100
  161.7 24.4 %all-gather.12 = f32[8,1,8192]{2,1,0:T(1,128)S(1)} all-gather(f32[1,1,8192]{2,1,0:T(1,128)S(1)} %reshape.82), channel_id=1, replica_groups=mesh['wide'=8,'narrow'=4] {'wide'}, dimensions={0}, use_global_device_ids=true | all-gather | bytes 294912 | tf_op jit(solution)/shard_map/all_gather | solution.py:13
  186.3 24.7 %all-gather.13 = f32[8,1,8192]{2,1,0:T(1,128)S(1)} all-gather(f32[1,1,8192]{2,1,0:T(1,128)S(1)} %reshape.84), channel_id=1, replica_groups=mesh['wide'=8,'narrow'=4] {'wide'}, dimensions={0}, use_global_device_ids=true | all-gather | bytes 294912 | tf_op jit(solution)/shard_map/all_gather | solution.py:13
  212.7 32.9 %while.170 = (s32[]{:T(128)}, f32[512]{0:T(512)S(1)}, f32[512]{0:T(512)S(1)}, bf16[4,2048,128]{2,1,0:T(8,128)(2,1)}, f32[4,2048]{1,0:T(4,128)S(1)}, /*index=5*/b...) while((s32[]{:T(128)}, f32[512]{0:T(512)S(1)}, ...), condition=%wide.region_29.30_spmd.clone, body=%wide.region_26.29_spmd.clone.sunk | while | flops 554699264 | bytes 31281820 | solution.py:113
  212.7 2.7 fusion.82
  215.4 3.1 exponential_reduce_fusion.14
  218.9 2.0 fusion.84
  220.9 2.7 fusion.82
  223.6 3.1 exponential_reduce_fusion.14
  227.1 2.1 fusion.84
  229.2 2.7 fusion.82
  231.9 3.1 exponential_reduce_fusion.14
  235.3 2.0 fusion.84
  237.4 2.7 fusion.82
  240.1 3.1 exponential_reduce_fusion.14
  243.6 2.1 fusion.84
  245.6 17.9 %all-gather.14 = f32[4,1,512]{2,1,0:T(1,128)S(1)} all-gather(f32[1,1,512]{2,1,0:T(1,128)S(1)} %bitcast.196), channel_id=6, replica_groups=mesh['wide'=8,'narrow'=4] {'narrow'}, dimensions={0}, use_global_device_ids=true | all-gather | bytes 10240 | tf_op jit(solution)/shard_map/all_gather | solution.py:13
  263.5 5.2 %all-gather.15 = f32[4,1,512]{2,1,0:T(1,128)S(1)} all-gather(f32[1,1,512]{2,1,0:T(1,128)S(1)} %bitcast.215), channel_id=7, replica_groups=mesh['wide'=8,'narrow'=4] {'narrow'}, dimensions={0}, use_global_device_ids=true | all-gather | bytes 10240 | tf_op jit(solution)/shard_map/all_gather | solution.py:13
  269.4 7.1 %while.171 = (s32[]{:T(128)}, f32[512,128]{1,0:T(8,128)S(1)}, f32[4,2048]{1,0:T(4,128)S(1)}, bf16[4,2048,128]{2,1,0:T(8,128)(2,1)S(1)}, bf16[512,128]{1,0:T(8,12...) while((s32[]{:T(128)}, f32[512,128]{1,0:T(8,128)S(1)}, f32[4,2048]{1,0:T(4,128)S(1)}, ...), condition=%wide.region_33.34_spmd.clone, body=%wide.region_32.33_spmd.clone.sunk | while | flops 543293440 | bytes 1731683 | solution.py:135
  277.8 30.1 %all-reduce.2.cloned.1.call-done = bf16[512,128]{1,0:T(8,128)(2,1)} async-done(((bf16[512,128]{1,0:T(8,128)(2,1)}), bf16[512,128]{1,0:T(8,128)(2,1)}) %all-reduce.2.cloned.1.call-update) | async-done | bytes 131088 | tf_op jit(solution)/shard_map/psum | solution.py:140
  309.6 39.5 %reduce-scatter.2.cloned.1.call-done = bf16[1024,128]{1,0:T(8,128)(2,1)} async-done(((bf16[8192,128]{1,0:T(8,128)(2,1)}), bf16[1024,128]{1,0:T(8,128)(2,1)}) %reduce-scatter.2.cloned.1.call-update) | async-done | bytes 262160 | tf_op jit(solution)/shard_map/reduce_scatter | solution.py:119
  (213 shorter events, 34.1 us)
Async XLA Ops:
  8.0 7.5 %copy-start.1 = (bf16[512,128]{1,0:T(8,128)(2,1)S(1)}, bf16[512,128]{1,0:T(8,128)(2,1)}, u32[]{:S(2)}) copy-start(bf16[512,128]{1,0:T(8,128)(2,1)} %param.27) | copy-start | bytes 393220
  8.0 7.8 %copy-start.4 = (f32[8192]{0:T(1024)S(1)}, f32[8192]{0:T(1024)}, u32[]{:S(2)}) copy-start(f32[8192]{0:T(1024)} %param.31) | copy-start | bytes 98308
  8.0 299.9 %all-reduce.2.cloned.1.call-start = ((), (), s32[]{:S(2)}) async-start(), calls=%async_computation.1 | async-start | bytes 262144 | tf_op jit(solution)/shard_map/psum | solution.py:140
  15.8 34.4 %copy-start.5 = (f32[512]{0:T(512)S(1)}, f32[512]{0:T(512)}, u32[]{:S(2)}) copy-start(f32[512]{0:T(512)} %param.29) | copy-start | bytes 6148
  50.3 58.1 %copy-start.3 = (f32[8192]{0:T(1024)S(1)}, f32[8192]{0:T(1024)}, u32[]{:S(2)}) copy-start(f32[8192]{0:T(1024)} %param.30) | copy-start | bytes 98308
  212.1 0.6 copy-start.2
  215.4 3.4 copy-start
  223.6 3.4 copy-start
  231.9 3.4 copy-start
  240.1 3.4 copy-start
  277.2 71.9 %reduce-scatter.2.cloned.1.call-start = ((), (), s32[]{:S(2)}) async-start(), calls=%async_computation.2 | async-start | bytes 2359296 | tf_op jit(solution)/shard_map/reduce_scatter | solution.py:119
Sparse Core Ops, SparseCore 0:
  277.3 30.5 all-reduce.1
Sparse Core Ops, SparseCore 1:
  281.2 67.8 reduce-scatter.1
where the time goes:
time: 361 us; the launch traced here: 358 us
  blocking collectives  156 us (43%)
  waiting for transfers between devices  70.1 us (19%)
  matrix products  55.3 us (15%)
  other arithmetic  53.4 us (15%)
  between operations  15.9 us (4%)
  local copies, waits for them, and re-layouts  6.07 us (2%)
    all_gather x10, blocking collectives, combined_all(): gathered = jax.tree.map(lambda a: lax.all_gather(a, axis), part)  156 us
    dot_general x20, matrix products, cost_of(): lax.dot_general(left, right, (((1,), (1,)), ((), ())), preferred_element_...  40.2 us
    reduce_scatter x1, waiting for transfers between devices, on_device(): lax.psum_scatter(tile_sums.reshape(n_cols, feat_width).astype(jnp.bfloat1...  39.5 us
    reduce_sum x12, other arithmetic, row_update(): jnp.sum(jnp.exp(scores - new_high[:, None]), axis=1)  34.8 us
    psum x1, waiting for transfers between devices, on_device(): sums_a = lax.psum(sums_a.astype(jnp.bfloat16), 'narrow').astype(jnp.float32)  30.1 us
    dot_general x4, matrix products, left_product(): lax.dot_general(weights, tile_a, (((0,), (0,)), ((), ())), preferred_elem...  8.2 us
  transfers between devices with their start and end apart: 2, of which 2 were waited for; matrix products, arithmetic and copies ran while one was open for 0% of the time, Pallas kernels for 0%

commit v1 on v0

v1 whole, which is shorter than its diff:
```python
import functools

import jax
import jax.numpy as jnp
from jax import lax
from jax.experimental import pallas as pl
from jax.experimental.pallas import tpu as pltpu
from jax.sharding import PartitionSpec as P

ITERS = 2
EPS = 0.05
SHIFT = 30.0
CENTRE = 2.0 / EPS
MESH = pl.DeviceIdType.MESH
NT = (((1,), (1,)), ((), ()))


def unit_of(desc):
    wide32 = desc.astype(jnp.float32)
    total = jnp.sum(wide32 * wide32, axis=1, keepdims=True) + 1e-06
    return (wide32 / jnp.sqrt(total)).astype(jnp.bfloat16)


def scaled_rows(logs, top):
    val = jnp.exp(logs - top + SHIFT)
    high = val.astype(jnp.bfloat16).astype(jnp.float32)
    low = val - high
    row = lax.broadcasted_iota(jnp.int32, (16, logs.shape[1]), 0)
    return val, jnp.where(row == 0, high, jnp.where(row == 1, low, 0.0)).astype(jnp.bfloat16)


def kernel(
    nw, nn,
    desc_a, desc_b, lm_a, lm_b, g_start,
    pot_a, pot_b, flow_a, flow_b,
    a_in, unit_a, unit_b, a_t, b_t, k_rows, k_cols, rows16, weighted,
    phi_in, psi_in, lse_in, flow_in, l_row, t_row, fsum,
    a_send, a_recv, phi_send, phi_recv, psi_send, psi_recv, lse_send, lse_recv, f_send, f_recv,
):
    wide = lax.axis_index("wide")
    narrow = lax.axis_index("narrow")
    rows, feat = desc_a.shape
    cols = desc_b.shape[0]
    share = cols // nw
    all_rows = nw * rows
    own_cols = pl.ds(pl.multiple_of(wide * share, share), share)
    own_rows = pl.ds(pl.multiple_of(wide * rows, rows), rows)

    barrier = pltpu.get_barrier_semaphore()
    for k in range(1, nw):
        pl.semaphore_signal(
            barrier, inc=1, device_id={"wide": lax.rem(wide + k, nw)}, device_id_type=MESH
        )
    for k in range(1, nn):
        pl.semaphore_signal(
            barrier, inc=1, device_id={"narrow": lax.rem(narrow + k, nn)}, device_id_type=MESH
        )

    def spread(axis, size, me, src, dst, send, recv):
        copies = []
        for k in range(1, size):
            copy = pltpu.make_async_remote_copy(
                src_ref=src, dst_ref=dst, send_sem=send.at[k], recv_sem=recv.at[k],
                device_id={axis: lax.rem(me + k, size)}, device_id_type=MESH,
            )
            copy.start()
            copies.append(copy)
        return copies

    def finish(copies):
        for copy in copies:
            copy.wait()

    own_unit = unit_of(desc_a[...])
    step_b = min(cols, 512)

    @pl.loop(0, cols // step_b)
    def _(c):
        at = pl.ds(pl.multiple_of(c * step_b, step_b), step_b)
        unit_b[at, :] = unit_of(desc_b[at, :])

    pl.semaphore_wait(barrier, nw + nn - 2)
    a_copies = spread("wide", nw, wide, desc_a, a_in.at[wide], a_send, a_recv)

    chunk = 256

    @pl.loop(0, cols // chunk)
    def _(c):
        at = pl.ds(pl.multiple_of(c * chunk, chunk), chunk)
        dots = lax.dot_general(unit_b[at, :], own_unit, NT, preferred_element_type=jnp.float32)
        k_cols[at, :] = jnp.exp(dots * CENTRE).astype(jnp.bfloat16)

    def log_sums(logs, mat, out):
        top = jnp.max(logs, axis=1, keepdims=True)
        val, pair = scaled_rows(logs, top)
        depth, width = mat.shape
        rows16[:, :depth] = pair
        block = min(width, 256)
        for c in range(width // block):
            at = pl.ds(c * block, block)
            got = jnp.dot(rows16[:, :depth], mat[:, at], preferred_element_type=jnp.float32)
            out[:, at] = jnp.log(got[0:1, :] + got[1:2, :]) + (top - SHIFT - CENTRE)
        return val, top

    def weighted_sums(val, tokens_t, mat, base, top, write):
        depth, width = mat.shape
        step = min(depth, 1024)
        for c in range(depth // step):
            at = pl.ds(c * step, step)
            part = tokens_t[:, at].astype(jnp.float32) * val[:, c * step:(c + 1) * step]
            weighted[:, at] = part.astype(jnp.bfloat16)
        block = min(width, 256)
        for c in range(width // block):
            at = pl.ds(c * block, block)
            got = jnp.dot(weighted[:, :depth], mat[:, at], preferred_element_type=jnp.float32)
            scale = jnp.exp((top - SHIFT - CENTRE) - base[:, at])
            write(at, got * scale)

    def joined(buf, t, n):
        return jnp.concatenate([buf[t, w] for w in range(n)], axis=1)

    def narrow_lse(t):
        parts = [lse_in[t, n] for n in range(nn)]
        top = functools.reduce(jnp.maximum, parts)
        return top + jnp.log(sum(jnp.exp(p - top) for p in parts))

    pending = []
    psi = g_start[...] / EPS
    for t in range(ITERS + 1):
        v_val, v_top = log_sums(psi, k_cols, l_row)
        lse_in[t, narrow] = l_row[...]
        lse_copies = spread(
            "narrow", nn, narrow, lse_in.at[t, narrow], lse_in.at[t, narrow],
            lse_send.at[t], lse_recv.at[t],
        )
        if t == ITERS:
            def put_a(at, value):
                flow_in[narrow, :, at] = value.astype(jnp.bfloat16)

            weighted_sums(v_val, b_t, k_cols, l_row, v_top, put_a)
            f_copies = spread(
                "narrow", nn, narrow, flow_in.at[narrow], flow_in.at[narrow], f_send, f_recv
            )
            finish(lse_copies)
            lse_a = narrow_lse(t)
            pot_a[...] = EPS * (lm_a[...] - lse_a)
            finish(f_copies)
            acc = jnp.zeros((feat, rows), jnp.float32)
            for n in range(nn):
                acc += flow_in[n].astype(jnp.float32) * jnp.exp(lse_in[t, n] - lse_a)
            flow_a[...] = acc.T - own_unit.astype(jnp.float32)
            break
        finish(lse_copies)
        phi_in[t, wide] = lm_a[...] - narrow_lse(t)
        phi_copies = spread(
            "wide", nw, wide, phi_in.at[t, wide], phi_in.at[t, wide],
            phi_send.at[t], phi_recv.at[t],
        )
        if t == 0:
            finish(a_copies)
            a_in[wide] = desc_a[...]

            for w in range(nw):
                unit_a[pl.ds(w * rows, rows), :] = unit_of(a_in[w])
            own_b = unit_b[own_cols, :]

            @pl.loop(0, all_rows // chunk)
            def _(c):
                at = pl.ds(pl.multiple_of(c * chunk, chunk), chunk)
                dots = lax.dot_general(unit_a[at, :], own_b, NT, preferred_element_type=jnp.float32)
                k_rows[at, :] = jnp.exp(dots * CENTRE).astype(jnp.bfloat16)

        finish(phi_copies)
        phi = joined(phi_in, t, nw)
        u_val, u_top = log_sums(phi, k_rows, t_row)
        psi_in[t, wide] = lm_b[:, own_cols] - t_row[...]
        psi_copies = spread(
            "wide", nw, wide, psi_in.at[t, wide], psi_in.at[t, wide],
            psi_send.at[t], psi_recv.at[t],
        )
        if t == 0:
            @pl.loop(0, cols // step_b)
            def _(c):
                at = pl.ds(pl.multiple_of(c * step_b, step_b), step_b)
                b_t[:, at] = unit_b[at, :].T

            for w in range(nw):
                at = pl.ds(w * rows, rows)
                a_t[:, at] = unit_a[at, :].T
        if t == ITERS - 1:
            def put_b(at, value):
                flow_b[at, :] = value.T - unit_b[
                    pl.ds(pl.multiple_of(wide * share + at.start, 128), at.size), :
                ].astype(jnp.float32)

            weighted_sums(u_val, a_t, k_rows, t_row, u_top, put_b)
        finish(psi_copies)
        psi = joined(psi_in, t, nw)
    pot_b[...] = EPS * psi


def on_device(desc_a, desc_b, logmass_a, logmass_b, g_start):
    nw = lax.axis_size("wide")
    nn = lax.axis_size("narrow")
    rows, feat = desc_a.shape
    cols = desc_b.shape[0]
    share = cols // nw
    all_rows = nw * rows
    longest = max(all_rows, cols)
    f32, bf16 = jnp.float32, jnp.bfloat16
    vmem = pltpu.VMEM
    dma = pltpu.SemaphoreType.DMA
    outs = pl.pallas_call(
        functools.partial(kernel, nw, nn),
        out_shape=(
            jax.ShapeDtypeStruct((1, rows), f32),
            jax.ShapeDtypeStruct((1, cols), f32),
            jax.ShapeDtypeStruct((rows, feat), f32),
            jax.ShapeDtypeStruct((share, feat), f32),
        ),
        in_specs=[pl.BlockSpec(memory_space=vmem)] * 5,
        out_specs=(pl.BlockSpec(memory_space=vmem),) * 4,
        scratch_shapes=[
            vmem((nw, rows, feat), bf16),
            vmem((all_rows, feat), bf16),
            vmem((cols, feat), bf16),
            vmem((feat, all_rows), bf16),
            vmem((feat, cols), bf16),
            vmem((all_rows, share), bf16),
            vmem((cols, rows), bf16),
            vmem((16, longest), bf16),
            vmem((feat, longest), bf16),
            vmem((ITERS, nw, 1, rows), f32),
            vmem((ITERS, nw, 1, share), f32),
            vmem((ITERS + 1, nn, 1, rows), f32),
            vmem((nn, feat, rows), bf16),
            vmem((1, rows), f32),
            vmem((1, share), f32),
            vmem((8, 128), f32),
            dma((nw,)), dma((nw,)),
            dma((ITERS, nw)), dma((ITERS, nw)),
            dma((ITERS, nw)), dma((ITERS, nw)),
            dma((ITERS + 1, nn)), dma((ITERS + 1, nn)),
            dma((nn,)), dma((nn,)),
        ],
        compiler_params=pltpu.CompilerParams(
            collective_id=0, has_side_effects=True, vmem_limit_bytes=60 * 1024 * 1024
        ),
        name="sinkhorn",
    )(
        desc_a, desc_b, logmass_a.reshape(1, rows), logmass_b.reshape(1, cols),
        g_start.reshape(1, cols),
    )
    return (outs[0].reshape(rows), outs[1].reshape(cols), outs[2], outs[3])


def solution(mesh):
    return jax.shard_map(
        on_device,
        mesh=mesh,
        in_specs=(P("wide", None), P("narrow", None), P("wide"), P("narrow"), P("narrow")),
        out_specs=(P("wide"), P("narrow"), P("wide", None), P(("narrow", "wide"), None)),
        check_vma=False,
    )
```

time: 361 us -> 73.6 us (0.20)
  blocking collectives: 156 us -> 0 us
  waiting for transfers between devices: 70.1 us -> 0 us
  Pallas kernels: 0 us -> 66.5 us
  matrix products: 55.3 us -> 0 us
  other arithmetic: 53.4 us -> 0 us
  between operations: 15.9 us -> 0.64 us
    all_gather x10 -> x0, blocking collectives: 156 us -> none  [combined_all(): gathered = jax.tree.map(lambda a: lax.all_gather(a, axis), part)]
    pallas_call x0 -> x1, Pallas kernels: none -> 66.5 us  [on_device(): pl.pallas_call(functools.partial(kernel, nw, nn), out_shape=(jax.ShapeDty...]
    dot_general x28 -> x0, matrix products: 55.3 us -> none  [the longest x20 40.2 us: cost_of(): lax.dot_general(left, right, (((1,), (1,)), ((), ())), preferred_element_...]
    reduce_sum x22 -> x0, other arithmetic: 42.8 us -> none  [the longest x12 34.8 us: row_update(): jnp.sum(jnp.exp(scores - new_high[:, None]), axis=1)]
    reduce_scatter x1 -> x0, waiting for transfers between devices: 39.5 us -> none  [on_device(): lax.psum_scatter(tile_sums.reshape(n_cols, feat_width).astype(jnp.bfloat1...]
    psum x1 -> x0, waiting for transfers between devices: 30.1 us -> none  [on_device(): sums_a = lax.psum(sums_a.astype(jnp.bfloat16), 'narrow').astype(jnp.float32)]
    convert_element_type x3 -> x0, other arithmetic: 5.43 us -> none  [the longest x2 4.76 us: unit_rows(): (wide32 / jnp.sqrt(jnp.sum(wide32 * wide32, axis=1, keepdims=True) + 1e-0...]
    unnamed x24 -> x4, local copies, waits for them, and re-layouts: 1.44 us -> 6.15 us
  transfers between devices with their start and end apart: 2 -> 0, of which waited for: 2 -> 0; matrix products, arithmetic and copies ran while one was open for 0% -> 0% of each run, Pallas kernels for 0% -> 0%
where the time goes in v1:
time: 73.6 us; the launch traced here: 73.3 us
  Pallas kernels  66.5 us (90%)
  local copies, waits for them, and re-layouts  6.15 us (8%)
    pallas_call x1, Pallas kernels, on_device(): pl.pallas_call(functools.partial(kernel, nw, nn), out_shape=(jax.ShapeDty...  66.5 us
    unnamed x4, local copies, waits for them, and re-layouts  6.15 us

profile of v1, /device:TPU:1, one launch (start us, length us, event | category | flops | bytes accessed | tf_op | source)
XLA Modules:
  0.0 73.3 jit_solution(8755386048539989157)
XLA Ops:
  0.6 66.5 %sinkhorn.1 = (f32[1,512]{1,0:T(1,128)}, f32[1,8192]{1,0:T(1,128)}, f32[512,128]{1,0:T(8,128)}, f32[1024,128]{1,0:T(8,128)}) custom-call(bf16[512,128]{1,0:T(8,128)(2,1)} %desc_a.1, bf16[8192,128]{1,0:T(8,128)(2,1)} %desc_b.1, f32[1,512]{1,0:T(1,128)} %bitcast.9, f32[1,8192]{1,0:T(1,128)} %bitcast.6, f32[1,8192]{1,0:T(1,128)} %bitcast.7), custom_call_target="tpu_custom_call" | custom-call | tf_op jit(solution)/shard_map/sinkhorn/pallas_call | solution.py:213
  67.1 1.2 %copy.13 = f32[512]{0:T(512)} copy(f32[512]{0:T(512)} %bitcast.8) | data formatting | bytes 4096
  68.3 1.4 %copy.14 = f32[8192]{0:T(1024)} copy(f32[8192]{0:T(1024)} %bitcast.5) | data formatting | bytes 65536
  69.7 1.7 %copy.15 = f32[512,128]{1,0:T(8,128)} copy(f32[512,128]{1,0:T(8,128)} %get-tuple-element.18) | data formatting | bytes 524288
  71.4 1.9 %copy.16 = f32[1024,128]{1,0:T(8,128)} copy(f32[1024,128]{1,0:T(8,128)} %get-tuple-element.19) | data formatting | bytes 1048576

commit v2 on v1

--- a/solution.py
+++ b/solution.py
@@ -11,6 +11,7 @@
 EPS = 0.05
 SHIFT = 30.0
 CENTRE = 2.0 / EPS
+LOG2E = 1.4426950408889634
 MESH = pl.DeviceIdType.MESH
 NT = (((1,), (1,)), ((), ()))
 
@@ -27,6 +28,13 @@
     low = val - high
     row = lax.broadcasted_iota(jnp.int32, (16, logs.shape[1]), 0)
     return val, jnp.where(row == 0, high, jnp.where(row == 1, low, 0.0)).astype(jnp.bfloat16)
+
+
+def scale_out(log_a, log_b, in_a, in_b, pot_a, pot_b, flow_a, flow_b):
+    pot_a[...] = EPS * log_a[...]
+    pot_b[...] = EPS * log_b[...]
+    flow_a[...] = in_a[...]
+    flow_b[...] = in_b[...]
 
 
 def kernel(
@@ -80,15 +88,42 @@
         unit_b[at, :] = unit_of(desc_b[at, :])
 
     pl.semaphore_wait(barrier, nw + nn - 2)
-    a_copies = spread("wide", nw, wide, desc_a, a_in.at[wide], a_send, a_recv)
+
+    half = rows // 2
+    side = lax.rem(narrow, 2)
+    mine = pl.ds(pl.multiple_of(side * half, half), half)
+    inner = lax.rem(wide, 2)
+    outer = lax.div(wide, 2)
+    n_outer = nw // 2
+
+    def block_of(k, flipped):
+        line = 1 - inner if flipped else inner
+        return lax.rem(outer - k + n_outer, n_outer) * 2 + line
+
+    def pass_on(src, block, slot, device):
+        copy = pltpu.make_async_remote_copy(
+            src_ref=src, dst_ref=a_in.at[block, mine], send_sem=a_send.at[slot],
+            recv_sem=a_recv.at[slot], device_id=device, device_id_type=MESH,
+        )
+        copy.start()
+        return copy
+
+    def to_line(k):
+        return {"wide": lax.rem(outer + k, n_outer) * 2 + inner}
+
+    to_next = {"wide": wide + 1 - 2 * inner}
+    to_twin = {"narrow": narrow + 1 - 2 * side}
+    along = [pass_on(desc_a.at[mine], wide, k, to_line(k)) for k in range(1, n_outer)]
+    across = [pass_on(desc_a.at[mine], wide, n_outer, to_next)]
+    twin = []
 
     chunk = 256
 
-    @pl.loop(0, cols // chunk)
+    @pl.loop(0, cols // chunk, unroll=4)
     def _(c):
         at = pl.ds(pl.multiple_of(c * chunk, chunk), chunk)
         dots = lax.dot_general(unit_b[at, :], own_unit, NT, preferred_element_type=jnp.float32)
-        k_cols[at, :] = jnp.exp(dots * CENTRE).astype(jnp.bfloat16)
+        k_cols[at, :] = jnp.exp2(dots * (CENTRE * LOG2E)).astype(jnp.bfloat16)
 
     def log_sums(logs, mat, out):
         top = jnp.max(logs, axis=1, keepdims=True)
@@ -143,13 +178,20 @@
             )
             finish(lse_copies)
             lse_a = narrow_lse(t)
-            pot_a[...] = EPS * (lm_a[...] - lse_a)
+            pot_a[...] = lm_a[...] - lse_a
             finish(f_copies)
             acc = jnp.zeros((feat, rows), jnp.float32)
             for n in range(nn):
                 acc += flow_in[n].astype(jnp.float32) * jnp.exp(lse_in[t, n] - lse_a)
             flow_a[...] = acc.T - own_unit.astype(jnp.float32)
             break
+        if t == 0:
+            for k in range(1, n_outer):
+                along[k - 1].wait_recv()
+                block = block_of(k, False)
+                src = a_in.at[block, mine]
+                across.append(pass_on(src, block, n_outer + k, to_next))
+                twin.append(pass_on(src, block, 2 * n_outer + k, to_twin))
         finish(lse_copies)
         phi_in[t, wide] = lm_a[...] - narrow_lse(t)
         phi_copies = spread(
@@ -157,18 +199,24 @@
             phi_send.at[t], phi_recv.at[t],
         )
         if t == 0:
-            finish(a_copies)
+            for k in range(n_outer):
+                across[k].wait_recv()
+                block = block_of(k, True)
+                twin.append(pass_on(a_in.at[block, mine], block, 3 * n_outer + k, to_twin))
+            for copy in along + across:
+                copy.wait_send()
+            finish(twin)
             a_in[wide] = desc_a[...]
 
             for w in range(nw):
                 unit_a[pl.ds(w * rows, rows), :] = unit_of(a_in[w])
             own_b = unit_b[own_cols, :]
 
-            @pl.loop(0, all_rows // chunk)
+            @pl.loop(0, all_rows // chunk, unroll=4)
             def _(c):
                 at = pl.ds(pl.multiple_of(c * chunk, chunk), chunk)
                 dots = lax.dot_general(unit_a[at, :], own_b, NT, preferred_element_type=jnp.float32)
-                k_rows[at, :] = jnp.exp(dots * CENTRE).astype(jnp.bfloat16)
+                k_rows[at, :] = jnp.exp2(dots * (CENTRE * LOG2E)).astype(jnp.bfloat16)
 
         finish(phi_copies)
         phi = joined(phi_in, t, nw)
@@ -196,7 +244,7 @@
             weighted_sums(u_val, a_t, k_rows, t_row, u_top, put_b)
         finish(psi_copies)
         psi = joined(psi_in, t, nw)
-    pot_b[...] = EPS * psi
+    pot_b[...] = psi
 
 
 def on_device(desc_a, desc_b, logmass_a, logmass_b, g_start):
@@ -237,7 +285,7 @@
             vmem((1, rows), f32),
             vmem((1, share), f32),
             vmem((8, 128), f32),
-            dma((nw,)), dma((nw,)),
+            dma((2 * nw,)), dma((2 * nw,)),
             dma((ITERS, nw)), dma((ITERS, nw)),
             dma((ITERS, nw)), dma((ITERS, nw)),
             dma((ITERS + 1, nn)), dma((ITERS + 1, nn)),
@@ -251,6 +299,13 @@
         desc_a, desc_b, logmass_a.reshape(1, rows), logmass_b.reshape(1, cols),
         g_start.reshape(1, cols),
     )
+    outs = pl.pallas_call(
+        scale_out,
+        out_shape=tuple(jax.ShapeDtypeStruct(o.shape, f32) for o in outs),
+        in_specs=[pl.BlockSpec(memory_space=vmem)] * 4,
+        out_specs=(pl.BlockSpec(memory_space=vmem),) * 4,
+        name="scale_out",
+    )(*outs)
     return (outs[0].reshape(rows), outs[1].reshape(cols), outs[2], outs[3])
 
 

time: 73.6 us -> 55.1 us (0.75)
  Pallas kernels: 66.5 us -> 54.3 us
  local copies, waits for them, and re-layouts: 6.15 us -> 0 us
    pallas_call x1, Pallas kernels: 66.5 us -> 52.3 us  [on_device(): pl.pallas_call(functools.partial(kernel, nw, nn), out_shape=(jax.ShapeDty...]
    unnamed x4 -> x0, local copies, waits for them, and re-layouts: 6.15 us -> none
    pallas_call x0 -> x1, Pallas kernels: none -> 2.05 us  [on_device(): pl.pallas_call(scale_out, out_shape=tuple((jax.ShapeDtypeStruct(o.shape,...]
where the time goes in v2:
time: 55.1 us; the launch traced here: 55 us
  Pallas kernels  54.3 us (99%)
  between operations  0.64 us (1%)
    pallas_call x1, Pallas kernels, on_device(): pl.pallas_call(functools.partial(kernel, nw, nn), out_shape=(jax.ShapeDty...  52.3 us
    pallas_call x1, Pallas kernels, on_device(): pl.pallas_call(scale_out, out_shape=tuple((jax.ShapeDtypeStruct(o.shape,...  2.05 us

profile of v2, /device:TPU:1, one launch (start us, length us, event | category | flops | bytes accessed | tf_op | source)
XLA Modules:
  0.0 55.0 jit_solution(15947215741330307840)
XLA Ops:
  0.6 52.3 %sinkhorn.1 = (f32[1,512]{1,0:T(1,128)}, f32[1,8192]{1,0:T(1,128)}, f32[512,128]{1,0:T(8,128)}, f32[1024,128]{1,0:T(8,128)}) custom-call(bf16[512,128]{1,0:T(8,128)(2,1)} %desc_a.1, bf16[8192,128]{1,0:T(8,128)(2,1)} %desc_b.1, f32[1,512]{1,0:T(1,128)} %bitcast.7, f32[1,8192]{1,0:T(1,128)} %bitcast.5, f32[1,8192]{1,0:T(1,128)} %bitcast.6), custom_call_target="tpu_custom_call" | custom-call | tf_op jit(solution)/shard_map/sinkhorn/pallas_call | solution.py:261
  52.9 2.0 %scale_out.1 = (f32[1,512]{1,0:T(1,128)}, f32[1,8192]{1,0:T(1,128)}, f32[512,128]{1,0:T(8,128)}, f32[1024,128]{1,0:T(8,128)}) custom-call(f32[1,512]{1,0:T(1,128)} %get-tuple-element.12.log_a, f32[1,8192]{1,0:T(1,128)} %get-tuple-element.13.log_b, f32[512,128]{1,0:T(8,128)} %get-tuple-element.14.in_a, f32[1024,128]{1,0:T(8,128)} %get-tuple-element.15.in_b), custom_call_target="tpu_custom_call" | custom-call | tf_op jit(solution)/shard_map/scale_out/pallas_call | solution.py:302
